TPU v7x, 512 devices: a whole 4x4x16 slice. The times are simulated.
512 devices in a mesh: dp: 8 (over y, x_lo), ctx: 64 (over z, x_hi, core).
Axes of the slice: x: 4 (x_hi: 2, x_lo: 2; x = x_hi * 2 + x_lo), y: 4, z: 16, core: 2. Of those that a mesh axis runs over, the one named last changes fastest.
Arguments:
- events: bfloat16 [8, 16384, 1024], P('dp', 'ctx'), may hold values from -6 to 6
- w_query: bfloat16 [1024, 512], replicated, may hold values from -0.1875 to 0.1875
- w_key: bfloat16 [1024, 512], replicated, may hold values from -0.1875 to 0.1875
- values: bfloat16 [8, 16384, 512], P('dp', 'ctx'), may hold values from -6 to 6
- grad_out: bfloat16 [8, 16384, 512], P('dp', 'ctx'), may hold values from -6 to 6
- lengths: int32 [8, 32], P('dp'), may hold values from 1 to 768, 16384 in all within a row
- stream_shift: int32 [8], P('dp'), may hold values from 0 to 16383
- block_keep: int32 [8, 128], P('dp'), may hold values 0 or 1
Outputs:
- attended: bfloat16 [8, 16384, 512], P('dp', 'ctx')
- grad_values: bfloat16 [8, 16384, 512], P('dp', 'ctx')
- grad_wq: bfloat16 [1024, 512], P('ctx')
- grad_wk: bfloat16 [1024, 512], P('ctx')
Inputs may be any that keep to these rules, and one draw needn't show every extreme that they name: The lengths of a stream sum to 16384; the longest is exactly 768.
All inputs are finite; a program needn't handle non-finite values. No bound on the sum of `block_keep` on one device may be relied on, other than what follows from the above.
Results may differ from a plain program's by a relative error of at most 0.011.
Values may be sent and summed in bfloat16 or wider, within the bound.
A program may use at most 64 MiB of HBM per device.

v0:
```python
import jax
import jax.numpy as jnp
from jax import lax
from jax.sharding import PartitionSpec as P

HD = 128
SPAN = 3
BLOCK = 128
MAXLEN = 768


def from_behind(value, axis, steps):
    count = lax.axis_size(axis)
    pairs = [(source, (source + steps) % count) for source in range(count)]
    return lax.ppermute(value, axis, pairs)


def tile_terms(query, grad, key, value, valid, scale, alpha):
    z = jnp.einsum("qhd,khd->hqk", query, key, preferred_element_type=jnp.float32) * alpha
    sig = jax.nn.sigmoid(z)
    weight = valid[None, :, :].astype(jnp.float32) * scale
    att = (z * sig * weight).astype(jnp.bfloat16)
    out = jnp.einsum("hqk,khd->qhd", att, value, preferred_element_type=jnp.float32)
    dprod = jnp.einsum("qhd,khd->hqk", grad, value, preferred_element_type=jnp.float32)
    dsc = (dprod * sig * (1.0 + z * (1.0 - sig)) * weight * alpha).astype(jnp.bfloat16)
    dquery = jnp.einsum("hqk,khd->qhd", dsc, key, preferred_element_type=jnp.float32)
    dkey = jnp.einsum("hqk,qhd->khd", dsc, query, preferred_element_type=jnp.float32)
    dvalue = jnp.einsum("hqk,qhd->khd", att, grad, preferred_element_type=jnp.float32)
    return (out, dquery, dkey, dvalue)


def body(events, w_query, w_key, values, grad_out, lengths, stream_shift, block_keep):
    rows = events.shape[1]
    features = w_query.shape[1]
    nheads = features // HD
    alpha = 1.0 / HD**0.5
    scale = 1.0 / MAXLEN**0.5
    local = events[0]
    queries = jnp.dot(local, w_query, preferred_element_type=jnp.float32).astype(jnp.bfloat16)
    keys = jnp.dot(local, w_key, preferred_element_type=jnp.float32).astype(jnp.bfloat16)
    queries = queries.reshape(rows, nheads, HD)
    keys = keys.reshape(rows, nheads, HD)
    vals = values[0].reshape(rows, nheads, HD)
    cotan = grad_out[0].reshape(rows, nheads, HD)
    cycle_size = lax.axis_size("ctx")
    myself = lax.axis_index("ctx")
    total = rows * cycle_size
    ends = jnp.cumsum(lengths[0])
    offset = stream_shift[0]
    keep = block_keep[0]
    blocks_all = jnp.arange(keep.shape[0], dtype=jnp.int32)
    within = jnp.arange(rows, dtype=jnp.int32)

    def describe(anchor):
        anchor = jnp.remainder(anchor, cycle_size)
        position = jnp.remainder(anchor * rows + within - offset, total)
        owner = jnp.sum((position[:, None] >= ends[None, :]).astype(jnp.int32), axis=1)
        which = position // BLOCK
        kept = (
            jnp.sum(jnp.where(which[:, None] == blocks_all[None, :], keep[None, :], 0), axis=1) > 0
        )
        return (position, owner, kept)

    zeros = jnp.zeros((rows, nheads, HD), jnp.float32)
    qinfo = describe(myself)
    moving = (keys, vals)
    carried = (zeros, zeros)
    out_acc = zeros
    dq_acc = zeros
    for step in range(SPAN + 1):
        if step > 0:
            moving = from_behind((moving[0], moving[1]), "ctx", 1)
            carried = (
                from_behind(carried[0].astype(jnp.bfloat16), "ctx", 1).astype(jnp.float32),
                from_behind(carried[1].astype(jnp.bfloat16), "ctx", 1).astype(jnp.float32),
            )
        kinfo = describe(myself - step)
        o, a, b, c = tile_terms(
            queries,
            cotan,
            moving[0],
            moving[1],
            (qinfo[1][:, None] == kinfo[1][None, :])
            & (kinfo[0][None, :] <= qinfo[0][:, None])
            & kinfo[2][None, :],
            scale,
            alpha,
        )
        out_acc = out_acc + o
        dq_acc = dq_acc + a
        carried = (carried[0] + b, carried[1] + c)
    carried = (
        from_behind(carried[0].astype(jnp.bfloat16), "ctx", -SPAN).astype(jnp.float32),
        from_behind(carried[1].astype(jnp.bfloat16), "ctx", -SPAN).astype(jnp.float32),
    )
    dk_acc, dv_acc = carried
    attended = out_acc.reshape(1, rows, features).astype(jnp.bfloat16)
    grad_values = dv_acc.reshape(1, rows, features).astype(jnp.bfloat16)
    dq_b = dq_acc.reshape(rows, features).astype(jnp.bfloat16)
    dk_b = dk_acc.reshape(rows, features).astype(jnp.bfloat16)
    joined = jnp.concatenate([dq_b, dk_b], axis=1)
    width_rows = local.shape[1]
    share = width_rows // cycle_size
    terms = jnp.einsum("rd,rf->df", local, joined, preferred_element_type=jnp.float32)
    summed = lax.psum(terms, ("dp", "ctx"))
    mine = lax.dynamic_slice_in_dim(summed, myself * share, share, 0)
    grad_wq = mine[:, :features].astype(jnp.bfloat16)
    grad_wk = mine[:, features:].astype(jnp.bfloat16)
    return (attended, grad_values, grad_wq, grad_wk)


def solution(mesh):
    placed = (
        P("dp", "ctx", None),
        P(),
        P(),
        P("dp", "ctx", None),
        P("dp", "ctx", None),
        P("dp", None),
        P("dp"),
        P("dp", None),
    )
    return jax.shard_map(
        body,
        mesh=mesh,
        in_specs=placed,
        out_specs=(P("dp", "ctx", None), P("dp", "ctx", None), P("ctx", None), P("ctx", None)),
        check_vma=False,
    )
```

profile of v0, /device:TPU:7, one launch (start us, length us, event | category | flops | bytes accessed | tf_op | source)
XLA Modules:
  0.0 291.1 jit_solution(15227647348382941098)
XLA Ops:
  0.6 1.2 copy.87
  1.8 4.9 %collective-permute-start.1 = (bf16[256,4,128]{0,2,1:T(8,128)(2,1)S(1)}, bf16[256,4,128]{0,2,1:T(8,128)(2,1)S(1)}, u32[]{:S(2)}, u32[]{:S(2)}) collective-permute-start(bf16[256,4,128]{0,2,1:T(8,128)(2,1)S(1)} %bitcast.101), channel_id=1, source_target_pairs={{0,1},{1,2},{2,3},{3,4},{4,5},{5,6},{6,7},{7,8},{8,9},{9,10},{10,1... | collective-permute-start | bytes 786440 | tf_op jit(solution)/shard_map/ppermute | solution.py:15
  6.8 1.5 fusion.20
  8.3 0.7 copy.157
  9.0 1.9 collective-permute-start
  11.7 1.0 select_reduce_fusion
  12.8 0.7 copy.86
  13.6 0.1 reduce
  13.7 1.0 reshape_squeeze.7
  14.8 1.8 convolution_convert_fusion.3
  16.6 0.1 copy.132
  16.7 0.1 convert_reduce_fusion
  16.8 1.2 and_select_fusion
  18.0 0.5 multiply_convert_fusion.3
  18.6 0.5 fusion.15
  19.1 1.0 fusion.19
  20.1 4.1 %collective-permute-start.10 = (bf16[256,4,128]{0,2,1:T(8,128)(2,1)}, bf16[256,4,128]{0,2,1:T(8,128)(2,1)}, u32[]{:S(2)}, u32[]{:S(2)}) collective-permute-start(bf16[256,4,128]{0,2,1:T(8,128)(2,1)} %fusion.19), channel_id=1, source_target_pairs={{0,1},{1,2},{2,3},{3,4},{4,5},{5,6},{6,7},{7,8},{8,9},{9,10},{10,1... | collective-permute-start | bytes 786440 | tf_op jit(solution)/shard_map/ppermute | solution.py:15
  24.2 1.1 fusion.18
  25.3 1.9 collective-permute-start.6
  27.2 0.3 fusion.44
  27.5 0.3 fusion.42
  27.8 1.6 multiply_convert_fusion.2
  29.4 0.5 fusion.14
  30.0 1.2 add_convert_fusion.2
  31.2 4.8 %collective-permute-start.11 = (bf16[256,4,128]{0,2,1:T(8,128)(2,1)S(1)}, bf16[256,4,128]{0,2,1:T(8,128)(2,1)S(1)}, u32[]{:S(2)}, u32[]{:S(2)}) collective-permute-start(bf16[256,4,128]{0,2,1:T(8,128)(2,1)S(1)} %add_convert_fusion.2), channel_id=1, source_target_pairs={{0,1},{1,2},{2,3},{3,4},{4,5},{5,6},{6,7},{7,8},{8,9},{9,10},{10,1... | collective-permute-start | bytes 786440 | tf_op jit(solution)/shard_map/ppermute | solution.py:15
  36.0 1.3 add_convert_fusion.5
  37.3 1.9 collective-permute-start.7
  39.2 4.1 %collective-permute-start.3 = (bf16[256,4,128]{0,2,1:T(8,128)(2,1)S(1)}, bf16[256,4,128]{0,2,1:T(8,128)(2,1)S(1)}, u32[]{:S(2)}, u32[]{:S(2)}) collective-permute-start(bf16[256,4,128]{0,2,1:T(8,128)(2,1)S(1)} %collective-permute-done.1), channel_id=1, source_target_pairs={{0,1},{1,2},{2,3},{3,4},{4,5},{5,6},{6,7},{7,8},{8,9},{9,10},{10,1... | collective-permute-start | bytes 786440 | tf_op jit(solution)/shard_map/ppermute | solution.py:15
  43.4 1.9 collective-permute-start.2
  45.3 0.3 convolution_add_fusion.5
  45.6 1.3 convolution_add_fusion.2
  46.9 2.7 collective-permute-done.2
  49.6 0.5 multiply_convert_fusion.1
  50.2 0.5 fusion.13
  50.7 0.2 convolution_bitcast_fusion.2
  51.0 6.7 %collective-permute-start.12 = (bf16[256,4,128]{0,2,1:T(8,128)(2,1)S(1)}, bf16[256,4,128]{0,2,1:T(8,128)(2,1)S(1)}, u32[]{:S(2)}, u32[]{:S(2)}) collective-permute-start(bf16[256,4,128]{0,2,1:T(8,128)(2,1)S(1)} %add_convert_fusion.1), channel_id=1, source_target_pairs={{0,1},{1,2},{2,3},{3,4},{4,5},{5,6},{6,7},{7,8},{8,9},{9,10},{10,1... | collective-permute-start | bytes 786440 | tf_op jit(solution)/shard_map/ppermute | solution.py:15
  57.7 0.3 convolution_bitcast_fusion.5
  58.1 0.7 add_convert_fusion.4
  58.8 1.9 collective-permute-start.8
  60.7 3.9 %collective-permute-start.5 = (bf16[256,4,128]{0,2,1:T(8,128)(2,1)S(1)}, bf16[256,4,128]{0,2,1:T(8,128)(2,1)S(1)}, u32[]{:S(2)}, u32[]{:S(2)}) collective-permute-start(bf16[256,4,128]{0,2,1:T(8,128)(2,1)S(1)} %collective-permute-done.3), channel_id=1, source_target_pairs={{0,1},{1,2},{2,3},{3,4},{4,5},{5,6},{6,7},{7,8},{8,9},{9,10},{10,1... | collective-permute-start | bytes 786440 | tf_op jit(solution)/shard_map/ppermute | solution.py:15
  64.6 1.9 collective-permute-start.4
  66.5 0.3 convolution_add_fusion.4
  66.9 0.3 convolution_add_fusion.1
  67.2 3.5 %collective-permute-done.4 = bf16[256,4,128]{2,0,1:T(8,128)(2,1)S(1)} collective-permute-done((bf16[256,4,128]{2,0,1:T(8,128)(2,1)S(1)}, bf16[256,4,128]{2,0,1:T(8,128)(2,1)S(1)}, u32[]{:S(2)}, u32[]{:S(2)}) %collective-permute-start.4) | collective-permute-done | bytes 262176 | tf_op jit(solution)/shard_map/ppermute | solution.py:15
  70.7 0.5 multiply_convert_fusion
  71.3 0.1 copy-done.5
  71.4 0.5 fusion.12
  72.0 0.2 convolution_bitcast_fusion.1
  72.2 1.0 fusion.16
  73.2 0.8 add_convert_fusion
  74.0 1.8 copy.117
  75.8 9.6 %collective-permute-start.13 = (bf16[256,4,128]{0,2,1:T(8,128)(2,1)}, bf16[256,4,128]{0,2,1:T(8,128)(2,1)}, u32[]{:S(2)}, u32[]{:S(2)}) collective-permute-start(bf16[256,4,128]{0,2,1:T(8,128)(2,1)} %add_convert_fusion), channel_id=1, source_target_pairs={{0,61},{1,62},{2,63},{3,0},{4,1},{5,2},{6,3},{7,4},{8,5},{9,6},{10... | collective-permute-start | bytes 786440 | tf_op jit(solution)/shard_map/ppermute | solution.py:15
  85.4 0.3 convolution_bitcast_fusion.4
  85.8 1.0 add_convert_fusion.3
  86.8 2.1 collective-permute-start.9
  88.9 1.3 fusion.17
  90.2 4.3 %collective-permute-done.9 = bf16[256,4,128]{2,0,1:T(8,128)(2,1)S(1)} collective-permute-done((bf16[256,4,128]{2,0,1:T(8,128)(2,1)S(1)}, bf16[256,4,128]{2,0,1:T(8,128)(2,1)S(1)}, u32[]{:S(2)}, u32[]{:S(2)}) %collective-permute-start.9) | collective-permute-done | bytes 262176 | tf_op jit(solution)/shard_map/ppermute | solution.py:15
  94.5 0.1 copy.100
  94.6 0.8 copy.118
  95.5 3.6 %convolution_bitcast_fusion = f32[1024,1024]{0,1:T(8,128)} fusion(bf16[256,512]{0,1:T(8,128)(2,1)} %bitcast.18, bf16[256,512]{0,1:T(8,128)(2,1)S(1)} %bitcast.104, bf16[1,256,1024]{2,1,0:T(8,128)(2,1)S(1)} %copy-done.1), kind=kOutput, calls=%fused_computation | convolution fusion | flops 537919488 | bytes 5242880 | tf_op jit(solution)/shard_map/rd,rf->df/dot_general | solution.py:104
  99.1 190.5 %all-reduce.1 = bf16[1024,1024]{0,1:T(8,128)(2,1)S(1)} all-reduce(f32[1024,1024]{0,1:T(8,128)} %convolution_bitcast_fusion), channel_id=1, replica_groups=mesh['dp'=8,'ctx'=64] {'dp','ctx'}, use_global_device_ids=true, to_apply=%region_9.10 | all-reduce | flops 1048576 | bytes 6291456 | tf_op jit(solution)/shard_map/psum | solution.py:105
  289.6 0.2 dynamic-slice_convert_fusion
  289.8 0.7 copy.120
  290.5 0.7 copy.119
  (33 shorter events, 0.3 us)
Async XLA Ops:
  0.6 6.2 %copy-start = (bf16[1024,512]{1,0:T(8,128)(2,1)S(1)}, bf16[1024,512]{1,0:T(8,128)(2,1)}, u32[]{:S(2)}) copy-start(bf16[1024,512]{1,0:T(8,128)(2,1)} %param.10) | copy-start | bytes 3145732
  1.8 27.6 %collective-permute-start.1 = (bf16[256,4,128]{0,2,1:T(8,128)(2,1)S(1)}, bf16[256,4,128]{0,2,1:T(8,128)(2,1)S(1)}, u32[]{:S(2)}, u32[]{:S(2)}) collective-permute-start(bf16[256,4,128]{0,2,1:T(8,128)(2,1)S(1)} %bitcast.101), channel_id=1, source_target_pairs={{0,1},{1,2},{2,3},{3,4},{4,5},{5,6},{6,7},{7,8},{8,9},{9,10},{10,1... | collective-permute-start | bytes 786440 | tf_op jit(solution)/shard_map/ppermute | solution.py:15
  9.0 18.8 %collective-permute-start = (bf16[256,4,128]{2,0,1:T(8,128)(2,1)}, bf16[256,4,128]{2,0,1:T(8,128)(2,1)}, u32[]{:S(2)}, u32[]{:S(2)}) collective-permute-start(bf16[256,4,128]{2,0,1:T(8,128)(2,1)} %bitcast.88), channel_id=1, source_target_pairs={{0,1},{1,2},{2,3},{3,4},{4,5},{5,6},{6,7},{7,8},{8,9},{9,10},{10,1... | collective-permute-start | bytes 786440 | tf_op jit(solution)/shard_map/ppermute | solution.py:15
  20.1 9.9 %collective-permute-start.10 = (bf16[256,4,128]{0,2,1:T(8,128)(2,1)}, bf16[256,4,128]{0,2,1:T(8,128)(2,1)}, u32[]{:S(2)}, u32[]{:S(2)}) collective-permute-start(bf16[256,4,128]{0,2,1:T(8,128)(2,1)} %fusion.19), channel_id=1, source_target_pairs={{0,1},{1,2},{2,3},{3,4},{4,5},{5,6},{6,7},{7,8},{8,9},{9,10},{10,1... | collective-permute-start | bytes 786440 | tf_op jit(solution)/shard_map/ppermute | solution.py:15
  25.3 10.7 %collective-permute-start.6 = (bf16[256,4,128]{2,0,1:T(8,128)(2,1)}, bf16[256,4,128]{2,0,1:T(8,128)(2,1)}, u32[]{:S(2)}, u32[]{:S(2)}) collective-permute-start(bf16[256,4,128]{2,0,1:T(8,128)(2,1)} %fusion.18), channel_id=1, source_target_pairs={{0,1},{1,2},{2,3},{3,4},{4,5},{5,6},{6,7},{7,8},{8,9},{9,10},{10,1... | collective-permute-start | bytes 786440 | tf_op jit(solution)/shard_map/ppermute | solution.py:15
  27.5 1.9 copy-start.4
  30.0 19.6 %copy-start.3 = (f32[256,256]{1,0:T(8,128)S(1)}, f32[256,256]{1,0:T(8,128)}, u32[]{:S(2)}) copy-start(f32[256,256]{1,0:T(8,128)} %get-tuple-element.27) | copy-start | bytes 786436
  31.2 19.7 %collective-permute-start.11 = (bf16[256,4,128]{0,2,1:T(8,128)(2,1)S(1)}, bf16[256,4,128]{0,2,1:T(8,128)(2,1)S(1)}, u32[]{:S(2)}, u32[]{:S(2)}) collective-permute-start(bf16[256,4,128]{0,2,1:T(8,128)(2,1)S(1)} %add_convert_fusion.2), channel_id=1, source_target_pairs={{0,1},{1,2},{2,3},{3,4},{4,5},{5,6},{6,7},{7,8},{8,9},{9,10},{10,1... | collective-permute-start | bytes 786440 | tf_op jit(solution)/shard_map/ppermute | solution.py:15
  37.3 20.8 %collective-permute-start.7 = (bf16[256,4,128]{2,0,1:T(8,128)(2,1)S(1)}, bf16[256,4,128]{2,0,1:T(8,128)(2,1)S(1)}, u32[]{:S(2)}, u32[]{:S(2)}) collective-permute-start(bf16[256,4,128]{2,0,1:T(8,128)(2,1)S(1)} %add_convert_fusion.5), channel_id=1, source_target_pairs={{0,1},{1,2},{2,3},{3,4},{4,5},{5,6},{6,7},{7,8},{8,9},{9,10},{10,1... | collective-permute-start | bytes 786440 | tf_op jit(solution)/shard_map/ppermute | solution.py:15
  39.2 10.9 %collective-permute-start.3 = (bf16[256,4,128]{0,2,1:T(8,128)(2,1)S(1)}, bf16[256,4,128]{0,2,1:T(8,128)(2,1)S(1)}, u32[]{:S(2)}, u32[]{:S(2)}) collective-permute-start(bf16[256,4,128]{0,2,1:T(8,128)(2,1)S(1)} %collective-permute-done.1), channel_id=1, source_target_pairs={{0,1},{1,2},{2,3},{3,4},{4,5},{5,6},{6,7},{7,8},{8,9},{9,10},{10,1... | collective-permute-start | bytes 786440 | tf_op jit(solution)/shard_map/ppermute | solution.py:15
  43.4 6.2 %collective-permute-start.2 = (bf16[256,4,128]{2,0,1:T(8,128)(2,1)}, bf16[256,4,128]{2,0,1:T(8,128)(2,1)S(1)}, u32[]{:S(2)}, u32[]{:S(2)}) collective-permute-start(bf16[256,4,128]{2,0,1:T(8,128)(2,1)} %collective-permute-done), channel_id=1, source_target_pairs={{0,1},{1,2},{2,3},{3,4},{4,5},{5,6},{6,7},{7,8},{8,9},{9,10},{10,1... | collective-permute-start | bytes 786440 | tf_op jit(solution)/shard_map/ppermute | solution.py:15
  50.7 20.0 %copy-start.2 = (f32[256,256]{1,0:T(8,128)S(1)}, f32[256,256]{1,0:T(8,128)}, u32[]{:S(2)}) copy-start(f32[256,256]{1,0:T(8,128)} %get-tuple-element.26) | copy-start | bytes 786436
  51.0 22.2 %collective-permute-start.12 = (bf16[256,4,128]{0,2,1:T(8,128)(2,1)S(1)}, bf16[256,4,128]{0,2,1:T(8,128)(2,1)S(1)}, u32[]{:S(2)}, u32[]{:S(2)}) collective-permute-start(bf16[256,4,128]{0,2,1:T(8,128)(2,1)S(1)} %add_convert_fusion.1), channel_id=1, source_target_pairs={{0,1},{1,2},{2,3},{3,4},{4,5},{5,6},{6,7},{7,8},{8,9},{9,10},{10,1... | collective-permute-start | bytes 786440 | tf_op jit(solution)/shard_map/ppermute | solution.py:15
  58.8 26.9 %collective-permute-start.8 = (bf16[256,4,128]{2,0,1:T(8,128)(2,1)}, bf16[256,4,128]{2,0,1:T(8,128)(2,1)}, u32[]{:S(2)}, u32[]{:S(2)}) collective-permute-start(bf16[256,4,128]{2,0,1:T(8,128)(2,1)} %add_convert_fusion.4), channel_id=1, source_target_pairs={{0,1},{1,2},{2,3},{3,4},{4,5},{5,6},{6,7},{7,8},{8,9},{9,10},{10,1... | collective-permute-start | bytes 786440 | tf_op jit(solution)/shard_map/ppermute | solution.py:15
  60.7 10.5 %collective-permute-start.5 = (bf16[256,4,128]{0,2,1:T(8,128)(2,1)S(1)}, bf16[256,4,128]{0,2,1:T(8,128)(2,1)S(1)}, u32[]{:S(2)}, u32[]{:S(2)}) collective-permute-start(bf16[256,4,128]{0,2,1:T(8,128)(2,1)S(1)} %collective-permute-done.3), channel_id=1, source_target_pairs={{0,1},{1,2},{2,3},{3,4},{4,5},{5,6},{6,7},{7,8},{8,9},{9,10},{10,1... | collective-permute-start | bytes 786440 | tf_op jit(solution)/shard_map/ppermute | solution.py:15
  64.6 6.1 %collective-permute-start.4 = (bf16[256,4,128]{2,0,1:T(8,128)(2,1)S(1)}, bf16[256,4,128]{2,0,1:T(8,128)(2,1)S(1)}, u32[]{:S(2)}, u32[]{:S(2)}) collective-permute-start(bf16[256,4,128]{2,0,1:T(8,128)(2,1)S(1)} %collective-permute-done.2), channel_id=1, source_target_pairs={{0,1},{1,2},{2,3},{3,4},{4,5},{5,6},{6,7},{7,8},{8,9},{9,10},{10,1... | collective-permute-start | bytes 786440 | tf_op jit(solution)/shard_map/ppermute | solution.py:15
  70.7 0.7 copy-start.5
  72.2 23.3 %copy-start.1 = (bf16[1,256,1024]{2,1,0:T(8,128)(2,1)S(1)}, bf16[1,256,1024]{2,1,0:T(8,128)(2,1)}, u32[]{:S(2)}) copy-start(bf16[1,256,1024]{2,1,0:T(8,128)(2,1)} %param.8) | copy-start | bytes 1572868
  75.8 19.7 %collective-permute-start.13 = (bf16[256,4,128]{0,2,1:T(8,128)(2,1)}, bf16[256,4,128]{0,2,1:T(8,128)(2,1)}, u32[]{:S(2)}, u32[]{:S(2)}) collective-permute-start(bf16[256,4,128]{0,2,1:T(8,128)(2,1)} %add_convert_fusion), channel_id=1, source_target_pairs={{0,61},{1,62},{2,63},{3,0},{4,1},{5,2},{6,3},{7,4},{8,5},{9,6},{10... | collective-permute-start | bytes 786440 | tf_op jit(solution)/shard_map/ppermute | solution.py:15
  86.8 7.7 %collective-permute-start.9 = (bf16[256,4,128]{2,0,1:T(8,128)(2,1)S(1)}, bf16[256,4,128]{2,0,1:T(8,128)(2,1)S(1)}, u32[]{:S(2)}, u32[]{:S(2)}) collective-permute-start(bf16[256,4,128]{2,0,1:T(8,128)(2,1)S(1)} %add_convert_fusion.3), channel_id=1, source_target_pairs={{0,61},{1,62},{2,63},{3,0},{4,1},{5,2},{6,3},{7,4},{8,5},{9,6},{10... | collective-permute-start | bytes 786440 | tf_op jit(solution)/shard_map/ppermute | solution.py:15
where the time goes:
time: 292 us; the launch traced here: 291 us
  blocking collectives  191 us (65%)
  starting transfers between devices  51.7 us (18%)
  matrix products  23 us (8%)
  waiting for transfers between devices  10.6 us (4%)
  local copies, waits for them, and re-layouts  8.31 us (3%)
  other arithmetic  5.18 us (2%)
    psum x1, blocking collectives, body(): summed = lax.psum(terms, ('dp', 'ctx'))  191 us
    ppermute x14, starting transfers between devices, from_behind(): return lax.ppermute(value, axis, pairs)  51.7 us
    ppermute x14, waiting for transfers between devices, from_behind(): return lax.ppermute(value, axis, pairs)  10.6 us
  transfers between devices with their start and end apart: 14, of which 3 were waited for; matrix products, arithmetic and copies ran while one was open for 10% of the time, Pallas kernels for 0%

commit v1 on v0

--- a/solution.py
+++ b/solution.py
@@ -102,7 +102,7 @@
     width_rows = local.shape[1]
     share = width_rows // cycle_size
     terms = jnp.einsum("rd,rf->df", local, joined, preferred_element_type=jnp.float32)
-    summed = lax.psum(terms, ("dp", "ctx"))
+    summed = lax.psum(lax.psum(terms, "dp"), "ctx")
     mine = lax.dynamic_slice_in_dim(summed, myself * share, share, 0)
     grad_wq = mine[:, :features].astype(jnp.bfloat16)
     grad_wk = mine[:, features:].astype(jnp.bfloat16)

time: 292 us -> 614 us (2.10); the launches traced: 291 us -> 603 us
  waiting for transfers between devices: 10.6 us -> 181 us
  blocking collectives: 191 us -> 298 us
  starting transfers between devices: 51.7 us -> 77.7 us
  between operations: 1.85 us -> 15.3 us
    psum x0 -> x1, waiting for transfers between devices: none -> 156 us  [body(): summed = lax.psum(lax.psum(terms, 'dp'), 'ctx')]
    psum x1, blocking collectives: 191 us -> 298 us  [body(): summed = lax.psum(lax.psum(terms, 'dp'), 'ctx')]
    ppermute x14, starting transfers between devices: 51.7 us -> 77.6 us  [from_behind(): return lax.ppermute(value, axis, pairs)]
    ppermute x14, waiting for transfers between devices: 10.6 us -> 24.9 us  [from_behind(): return lax.ppermute(value, axis, pairs)]
  transfers between devices with their start and end apart: 14 -> 15, of which waited for: 3 -> 9; matrix products, arithmetic and copies ran while one was open for 10% -> 4% of each run, Pallas kernels for 0% -> 0%
where the time goes in v1:
time: 614 us; the launch traced here: 603 us
  blocking collectives  298 us (49%)
  waiting for transfers between devices  181 us (29%)
  starting transfers between devices  77.7 us (13%)
  matrix products  21.6 us (4%)
  between operations  15.3 us (2%)
  local copies, waits for them, and re-layouts  7.24 us (1%)
    psum x1, blocking collectives, body(): summed = lax.psum(lax.psum(terms, 'dp'), 'ctx')  298 us
    psum x1, waiting for transfers between devices, body(): summed = lax.psum(lax.psum(terms, 'dp'), 'ctx')  156 us
    ppermute x14, starting transfers between devices, from_behind(): return lax.ppermute(value, axis, pairs)  77.6 us
    ppermute x14, waiting for transfers between devices, from_behind(): return lax.ppermute(value, axis, pairs)  24.9 us
  transfers between devices with their start and end apart: 15, of which 9 were waited for; matrix products, arithmetic and copies ran while one was open for 4% of the time, Pallas kernels for 0%

profile of v1, /device:TPU:7, one launch (start us, length us, event | category | flops | bytes accessed | tf_op | source)
XLA Modules:
  0.0 603.2 jit_solution(7987297032252595614)
XLA Ops:
  7.2 1.2 copy.87
  8.4 4.9 collective-permute-start.1
  13.4 1.5 fusion.20
  14.9 0.7 copy.157
  15.6 1.9 collective-permute-start
  18.3 1.0 select_reduce_fusion
  19.4 0.7 copy.86
  20.3 1.0 reshape_squeeze.7
  21.3 1.8 convolution_convert_fusion.3
  23.4 0.3 and_select_fusion
  23.7 1.4 multiply_convert_fusion.3
  25.1 0.5 fusion.15
  25.7 0.2 fusion.19
  25.9 4.1 collective-permute-start.10
  30.0 0.3 fusion.42
  30.4 1.5 multiply_convert_fusion.2
  31.9 0.5 fusion.14
  32.4 0.9 collective-permute-done.10
  33.3 0.2 add_convert_fusion.2
  33.6 6.8 %collective-permute-start.11 = (bf16[256,4,128]{0,2,1:T(8,128)(2,1)S(1)}, bf16[256,4,128]{0,2,1:T(8,128)(2,1)S(1)}, u32[]{:S(2)}, u32[]{:S(2)}) collective-permute-start(bf16[256,4,128]{0,2,1:T(8,128)(2,1)S(1)} %add_convert_fusion.2), channel_id=1, source_target_pairs={{0,1},{1,2},{2,3},{3,4},{4,5},{5,6},{6,7},{7,8},{8,9},{9,10},{10,1... | collective-permute-start | bytes 786440 | tf_op jit(solution)/shard_map/ppermute | solution.py:15
  40.4 1.9 collective-permute-start.3
  42.3 3.9 collective-permute-start.2
  46.2 1.3 convolution_add_fusion.2
  47.5 2.3 collective-permute-done.2
  49.8 0.5 multiply_convert_fusion.1
  50.4 0.5 fusion.13
  50.9 0.2 convolution_bitcast_fusion.2
  51.2 6.7 %collective-permute-start.12 = (bf16[256,4,128]{0,2,1:T(8,128)(2,1)S(1)}, bf16[256,4,128]{0,2,1:T(8,128)(2,1)S(1)}, u32[]{:S(2)}, u32[]{:S(2)}) collective-permute-start(bf16[256,4,128]{0,2,1:T(8,128)(2,1)S(1)} %add_convert_fusion.1), channel_id=1, source_target_pairs={{0,1},{1,2},{2,3},{3,4},{4,5},{5,6},{6,7},{7,8},{8,9},{9,10},{10,1... | collective-permute-start | bytes 786440 | tf_op jit(solution)/shard_map/ppermute | solution.py:15
  57.9 1.9 collective-permute-start.5
  59.9 4.1 collective-permute-start.4
  64.0 0.3 convolution_add_fusion.1
  64.3 3.0 collective-permute-done.4
  67.3 0.5 multiply_convert_fusion
  67.9 0.5 fusion.12
  68.4 0.2 convolution_bitcast_fusion.1
  68.7 11.1 %collective-permute-start.13 = (bf16[256,4,128]{0,2,1:T(8,128)(2,1)S(1)}, bf16[256,4,128]{0,2,1:T(8,128)(2,1)S(1)}, u32[]{:S(2)}, u32[]{:S(2)}) collective-permute-start(bf16[256,4,128]{0,2,1:T(8,128)(2,1)S(1)} %add_convert_fusion), channel_id=1, source_target_pairs={{0,61},{1,62},{2,63},{3,0},{4,1},{5,2},{6,3},{7,4},{8,5},{9,6},{10... | collective-permute-start | bytes 786440 | tf_op jit(solution)/shard_map/ppermute | solution.py:15
  79.9 0.3 fusion.17
  80.2 3.0 collective-permute-done.13
  83.2 2.7 convolution_bitcast_fusion
  85.9 2.1 fusion.18
  88.0 1.9 collective-permute-start.6
  90.0 1.4 fusion.44
  91.4 2.2 collective-permute-done.6
  93.6 1.3 add_convert_fusion.5
  94.9 6.9 %collective-permute-start.7 = (bf16[256,4,128]{2,0,1:T(8,128)(2,1)S(1)}, bf16[256,4,128]{2,0,1:T(8,128)(2,1)S(1)}, u32[]{:S(2)}, u32[]{:S(2)}) collective-permute-start(bf16[256,4,128]{2,0,1:T(8,128)(2,1)S(1)} %add_convert_fusion.5), channel_id=1, source_target_pairs={{0,1},{1,2},{2,3},{3,4},{4,5},{5,6},{6,7},{7,8},{8,9},{9,10},{10,1... | collective-permute-start | bytes 786440 | tf_op jit(solution)/shard_map/ppermute | solution.py:15
  101.8 0.3 convolution_add_fusion.5
  102.1 0.3 convolution_bitcast_fusion.5
  102.5 2.6 collective-permute-done.7
  105.2 6.8 %collective-permute-start.8 = (bf16[256,4,128]{2,0,1:T(8,128)(2,1)S(1)}, bf16[256,4,128]{2,0,1:T(8,128)(2,1)S(1)}, u32[]{:S(2)}, u32[]{:S(2)}) collective-permute-start(bf16[256,4,128]{2,0,1:T(8,128)(2,1)S(1)} %add_convert_fusion.4), channel_id=1, source_target_pairs={{0,1},{1,2},{2,3},{3,4},{4,5},{5,6},{6,7},{7,8},{8,9},{9,10},{10,1... | collective-permute-start | bytes 786440 | tf_op jit(solution)/shard_map/ppermute | solution.py:15
  112.0 0.3 convolution_add_fusion.4
  112.3 0.3 convolution_bitcast_fusion.4
  112.6 2.7 collective-permute-done.8
  115.3 0.8 add_convert_fusion.3
  116.1 14.5 %collective-permute-start.9 = (bf16[256,4,128]{2,0,1:T(8,128)(2,1)}, bf16[256,4,128]{2,0,1:T(8,128)(2,1)S(1)}, u32[]{:S(2)}, u32[]{:S(2)}) collective-permute-start(bf16[256,4,128]{2,0,1:T(8,128)(2,1)} %add_convert_fusion.3), channel_id=1, source_target_pairs={{0,61},{1,62},{2,63},{3,0},{4,1},{5,2},{6,3},{7,4},{8,5},{9,6},{10... | collective-permute-start | bytes 786440 | tf_op jit(solution)/shard_map/ppermute | solution.py:15
  130.6 0.3 fusion.16
  130.9 0.8 copy.117
  131.8 8.2 %collective-permute-done.9 = bf16[256,4,128]{2,0,1:T(8,128)(2,1)S(1)} collective-permute-done((bf16[256,4,128]{2,0,1:T(8,128)(2,1)}, bf16[256,4,128]{2,0,1:T(8,128)(2,1)S(1)}, u32[]{:S(2)}, u32[]{:S(2)}) %collective-permute-start.9) | collective-permute-done | bytes 262176 | tf_op jit(solution)/shard_map/ppermute | solution.py:15
  140.0 0.1 copy.100
  140.2 0.8 copy.118
  141.0 156.0 %all-reduce.3.cloned.1.call-done = f32[1024,1024]{0,1:T(8,128)} async-done(((f32[1024,1024]{0,1:T(8,128)}), f32[1024,1024]{0,1:T(8,128)}) %all-reduce.3.cloned.1.call-update) | async-done | bytes 4194320 | tf_op jit(solution)/shard_map/psum | solution.py:105
  297.0 297.8 %all-reduce.4 = bf16[1024,1024]{0,1:T(8,128)(2,1)S(1)} all-reduce(f32[1024,1024]{0,1:T(8,128)} %all-reduce.3.cloned.1.call-done), channel_id=1, replica_groups=mesh['dp'=8,'ctx'=64] {'ctx'}, use_global_device_ids=true, to_apply=%region_10.11 | all-reduce | flops 1048576 | bytes 6291456 | tf_op jit(solution)/shard_map/psum | solution.py:105
  594.8 0.2 dynamic-slice_convert_fusion
  595.0 0.7 copy.120
  595.7 0.7 copy.119
  (44 shorter events, 0.8 us)
Async XLA Ops:
  7.2 6.2 %copy-start = (bf16[1024,512]{1,0:T(8,128)(2,1)S(1)}, bf16[1024,512]{1,0:T(8,128)(2,1)}, u32[]{:S(2)}) copy-start(bf16[1024,512]{1,0:T(8,128)(2,1)} %param.10) | copy-start | bytes 3145732
  7.2 289.8 %all-reduce.3.cloned.1.call-start = ((), (), s32[]{:S(2)}) async-start(), calls=%async_computation | async-start | bytes 8388608 | tf_op jit(solution)/shard_map/psum | solution.py:105
  8.4 16.7 %copy-start.2 = (bf16[1,256,512]{1,2,0:T(8,128)(2,1)}, bf16[1,256,512]{1,2,0:T(8,128)(2,1)S(1)}, u32[]{:S(2)}) copy-start(bf16[1,256,512]{1,2,0:T(8,128)(2,1)S(1)} %copy.87) | copy-start | bytes 786436
  8.4 23.5 %collective-permute-start.1 = (bf16[256,4,128]{0,2,1:T(8,128)(2,1)S(1)}, bf16[256,4,128]{0,2,1:T(8,128)(2,1)S(1)}, u32[]{:S(2)}, u32[]{:S(2)}) collective-permute-start(bf16[256,4,128]{0,2,1:T(8,128)(2,1)S(1)} %bitcast.101), channel_id=1, source_target_pairs={{0,1},{1,2},{2,3},{3,4},{4,5},{5,6},{6,7},{7,8},{8,9},{9,10},{10,1... | collective-permute-start | bytes 786440 | tf_op jit(solution)/shard_map/ppermute | solution.py:15
  15.6 14.8 %collective-permute-start = (bf16[256,4,128]{2,0,1:T(8,128)(2,1)}, bf16[256,4,128]{2,0,1:T(8,128)(2,1)}, u32[]{:S(2)}, u32[]{:S(2)}) collective-permute-start(bf16[256,4,128]{2,0,1:T(8,128)(2,1)} %bitcast.88), channel_id=1, source_target_pairs={{0,1},{1,2},{2,3},{3,4},{4,5},{5,6},{6,7},{7,8},{8,9},{9,10},{10,1... | collective-permute-start | bytes 786440 | tf_op jit(solution)/shard_map/ppermute | solution.py:15
  25.9 7.4 %collective-permute-start.10 = (bf16[256,4,128]{0,2,1:T(8,128)(2,1)S(1)}, bf16[256,4,128]{0,2,1:T(8,128)(2,1)S(1)}, u32[]{:S(2)}, u32[]{:S(2)}) collective-permute-start(bf16[256,4,128]{0,2,1:T(8,128)(2,1)S(1)} %fusion.19), channel_id=1, source_target_pairs={{0,1},{1,2},{2,3},{3,4},{4,5},{5,6},{6,7},{7,8},{8,9},{9,10},{10,1... | collective-permute-start | bytes 786440 | tf_op jit(solution)/shard_map/ppermute | solution.py:15
  31.9 15.6 %copy-start.4 = (bf16[256,4,128]{0,2,1:T(8,128)(2,1)}, bf16[256,4,128]{0,2,1:T(8,128)(2,1)S(1)}, u32[]{:S(2)}) copy-start(bf16[256,4,128]{0,2,1:T(8,128)(2,1)S(1)} %collective-permute-done.1) | copy-start | bytes 786436
  33.6 17.6 %collective-permute-start.11 = (bf16[256,4,128]{0,2,1:T(8,128)(2,1)S(1)}, bf16[256,4,128]{0,2,1:T(8,128)(2,1)S(1)}, u32[]{:S(2)}, u32[]{:S(2)}) collective-permute-start(bf16[256,4,128]{0,2,1:T(8,128)(2,1)S(1)} %add_convert_fusion.2), channel_id=1, source_target_pairs={{0,1},{1,2},{2,3},{3,4},{4,5},{5,6},{6,7},{7,8},{8,9},{9,10},{10,1... | collective-permute-start | bytes 786440 | tf_op jit(solution)/shard_map/ppermute | solution.py:15
  40.4 10.0 %collective-permute-start.3 = (bf16[256,4,128]{0,2,1:T(8,128)(2,1)S(1)}, bf16[256,4,128]{0,2,1:T(8,128)(2,1)S(1)}, u32[]{:S(2)}, u32[]{:S(2)}) collective-permute-start(bf16[256,4,128]{0,2,1:T(8,128)(2,1)S(1)} %collective-permute-done.1), channel_id=1, source_target_pairs={{0,1},{1,2},{2,3},{3,4},{4,5},{5,6},{6,7},{7,8},{8,9},{9,10},{10,1... | collective-permute-start | bytes 786440 | tf_op jit(solution)/shard_map/ppermute | solution.py:15
  42.3 7.5 %collective-permute-start.2 = (bf16[256,4,128]{2,0,1:T(8,128)(2,1)}, bf16[256,4,128]{2,0,1:T(8,128)(2,1)S(1)}, u32[]{:S(2)}, u32[]{:S(2)}) collective-permute-start(bf16[256,4,128]{2,0,1:T(8,128)(2,1)} %collective-permute-done), channel_id=1, source_target_pairs={{0,1},{1,2},{2,3},{3,4},{4,5},{5,6},{6,7},{7,8},{8,9},{9,10},{10,1... | collective-permute-start | bytes 786440 | tf_op jit(solution)/shard_map/ppermute | solution.py:15
  50.4 7.6 %copy-start.6 = (bf16[256,4,128]{0,2,1:T(8,128)(2,1)}, bf16[256,4,128]{0,2,1:T(8,128)(2,1)S(1)}, u32[]{:S(2)}) copy-start(bf16[256,4,128]{0,2,1:T(8,128)(2,1)S(1)} %collective-permute-done.3) | copy-start | bytes 786436
  51.2 17.4 %collective-permute-start.12 = (bf16[256,4,128]{0,2,1:T(8,128)(2,1)S(1)}, bf16[256,4,128]{0,2,1:T(8,128)(2,1)S(1)}, u32[]{:S(2)}, u32[]{:S(2)}) collective-permute-start(bf16[256,4,128]{0,2,1:T(8,128)(2,1)S(1)} %add_convert_fusion.1), channel_id=1, source_target_pairs={{0,1},{1,2},{2,3},{3,4},{4,5},{5,6},{6,7},{7,8},{8,9},{9,10},{10,1... | collective-permute-start | bytes 786440 | tf_op jit(solution)/shard_map/ppermute | solution.py:15
  57.9 9.9 %collective-permute-start.5 = (bf16[256,4,128]{0,2,1:T(8,128)(2,1)S(1)}, bf16[256,4,128]{0,2,1:T(8,128)(2,1)S(1)}, u32[]{:S(2)}, u32[]{:S(2)}) collective-permute-start(bf16[256,4,128]{0,2,1:T(8,128)(2,1)S(1)} %collective-permute-done.3), channel_id=1, source_target_pairs={{0,1},{1,2},{2,3},{3,4},{4,5},{5,6},{6,7},{7,8},{8,9},{9,10},{10,1... | collective-permute-start | bytes 786440 | tf_op jit(solution)/shard_map/ppermute | solution.py:15
  59.9 7.4 %collective-permute-start.4 = (bf16[256,4,128]{2,0,1:T(8,128)(2,1)S(1)}, bf16[256,4,128]{2,0,1:T(8,128)(2,1)S(1)}, u32[]{:S(2)}, u32[]{:S(2)}) collective-permute-start(bf16[256,4,128]{2,0,1:T(8,128)(2,1)S(1)} %collective-permute-done.2), channel_id=1, source_target_pairs={{0,1},{1,2},{2,3},{3,4},{4,5},{5,6},{6,7},{7,8},{8,9},{9,10},{10,1... | collective-permute-start | bytes 786440 | tf_op jit(solution)/shard_map/ppermute | solution.py:15
  67.9 0.8 copy-start.8
  67.9 15.3 %copy-start.1 = (bf16[1,256,1024]{2,1,0:T(8,128)(2,1)S(1)}, bf16[1,256,1024]{2,1,0:T(8,128)(2,1)}, u32[]{:S(2)}) copy-start(bf16[1,256,1024]{2,1,0:T(8,128)(2,1)} %param.8) | copy-start | bytes 1572868
  68.7 14.4 %collective-permute-start.13 = (bf16[256,4,128]{0,2,1:T(8,128)(2,1)S(1)}, bf16[256,4,128]{0,2,1:T(8,128)(2,1)S(1)}, u32[]{:S(2)}, u32[]{:S(2)}) collective-permute-start(bf16[256,4,128]{0,2,1:T(8,128)(2,1)S(1)} %add_convert_fusion), channel_id=1, source_target_pairs={{0,61},{1,62},{2,63},{3,0},{4,1},{5,2},{6,3},{7,4},{8,5},{9,6},{10... | collective-permute-start | bytes 786440 | tf_op jit(solution)/shard_map/ppermute | solution.py:15
  85.9 4.1 copy-start.3
  85.9 15.9 %copy-start.5 = (bf16[256,4,128]{0,2,1:T(8,128)(2,1)S(1)}, bf16[256,4,128]{0,2,1:T(8,128)(2,1)}, u32[]{:S(2)}) copy-start(bf16[256,4,128]{0,2,1:T(8,128)(2,1)} %copy-done.4) | copy-start | bytes 786436
  88.0 5.5 collective-permute-start.6
  90.0 22.0 %copy-start.7 = (bf16[256,4,128]{0,2,1:T(8,128)(2,1)S(1)}, bf16[256,4,128]{0,2,1:T(8,128)(2,1)}, u32[]{:S(2)}) copy-start(bf16[256,4,128]{0,2,1:T(8,128)(2,1)} %copy-done.6) | copy-start | bytes 786436
  94.9 35.8 %copy-start.9 = (bf16[256,4,128]{0,2,1:T(8,128)(2,1)S(1)}, bf16[256,4,128]{0,2,1:T(8,128)(2,1)}, u32[]{:S(2)}) copy-start(bf16[256,4,128]{0,2,1:T(8,128)(2,1)} %copy-done.8) | copy-start | bytes 786436
  94.9 10.2 %collective-permute-start.7 = (bf16[256,4,128]{2,0,1:T(8,128)(2,1)S(1)}, bf16[256,4,128]{2,0,1:T(8,128)(2,1)S(1)}, u32[]{:S(2)}, u32[]{:S(2)}) collective-permute-start(bf16[256,4,128]{2,0,1:T(8,128)(2,1)S(1)} %add_convert_fusion.5), channel_id=1, source_target_pairs={{0,1},{1,2},{2,3},{3,4},{4,5},{5,6},{6,7},{7,8},{8,9},{9,10},{10,1... | collective-permute-start | bytes 786440 | tf_op jit(solution)/shard_map/ppermute | solution.py:15
  105.2 10.1 %collective-permute-start.8 = (bf16[256,4,128]{2,0,1:T(8,128)(2,1)S(1)}, bf16[256,4,128]{2,0,1:T(8,128)(2,1)S(1)}, u32[]{:S(2)}, u32[]{:S(2)}) collective-permute-start(bf16[256,4,128]{2,0,1:T(8,128)(2,1)S(1)} %add_convert_fusion.4), channel_id=1, source_target_pairs={{0,1},{1,2},{2,3},{3,4},{4,5},{5,6},{6,7},{7,8},{8,9},{9,10},{10,1... | collective-permute-start | bytes 786440 | tf_op jit(solution)/shard_map/ppermute | solution.py:15
  116.1 23.9 %collective-permute-start.9 = (bf16[256,4,128]{2,0,1:T(8,128)(2,1)}, bf16[256,4,128]{2,0,1:T(8,128)(2,1)S(1)}, u32[]{:S(2)}, u32[]{:S(2)}) collective-permute-start(bf16[256,4,128]{2,0,1:T(8,128)(2,1)} %add_convert_fusion.3), channel_id=1, source_target_pairs={{0,61},{1,62},{2,63},{3,0},{4,1},{5,2},{6,3},{7,4},{8,5},{9,6},{10... | collective-permute-start | bytes 786440 | tf_op jit(solution)/shard_map/ppermute | solution.py:15
Sparse Core Ops, SparseCore 0:
  86.0 210.9 all-reduce.2
